TPU v7x, 32 devices: a whole 2x2x4 slice. The times are simulated.
32 devices in a mesh: dp: 4 (over z), seq: 8 (over y, x, core).
Axes of the slice: x: 2, y: 2, z: 4, core: 2. Of those that a mesh axis runs over, the one named last changes fastest.
Arguments:
- patches: bfloat16 [6144, 1280], P(('dp', 'seq')), may hold values from -6 to 6
- query_key_value: bfloat16 [6144, 3840], P(('dp', 'seq')), may hold values from -100 to 100
- counts: int32 [32, 4], P(('dp', 'seq')), may hold values from 4 to 48, as said below
- owner_index: int32 [1536, 1], P(('dp', 'seq')), may hold values from 0 to 7; in each aligned block of 48 rows (0 to 47, 48 to 95, ...) at most 6 rows name the same one
- out_weight: bfloat16 [1280, 1280], P(None, 'dp'), may hold values from -0.15625 to 0.15625
- ln_gain: float32 [1280], replicated, may hold values from 0.25 to 1.75
- ln_bias: float32 [1280], replicated, may hold values from -3 to 3
Outputs:
- image_tokens: bfloat16 [1536, 5120], P(('dp', 'seq'))
Inputs may be any that keep to these rules, and one draw needn't show every extreme that they name: Every count is a multiple of 4, each device's counts sum to at most 192, and some device's counts sum to exactly 192. `owner_index`: among the merge groups of one device, at most 6 name the same owner.
All inputs are finite; a program needn't handle non-finite values.
Results may differ from a plain program's by a relative error of at most 0.0029.
Values may be sent and summed in bfloat16 or wider, within the bound.
A program may use at most 64 MiB of HBM per device.

v0:
```python
import jax
import jax.numpy as jnp
from jax import lax
from jax.sharding import PartitionSpec as P

HEADS = 16
IMGS = 4


def segment_rows(count_row, row_count):
    image_ends = jnp.cumsum(count_row)
    row_ids = jnp.arange(row_count, dtype=jnp.int32)
    return jnp.sum((row_ids[:, None] >= image_ends[None, :]).astype(jnp.int32), axis=1)


def attend(packed, segment_ids, model_width):
    row_count = packed.shape[0]
    head_size = model_width // HEADS
    queries = packed[:, :model_width].reshape(row_count, HEADS, head_size)
    keys_all = packed[:, model_width : 2 * model_width].reshape(row_count, HEADS, head_size)
    values_all = packed[:, 2 * model_width :].reshape(row_count, HEADS, head_size)
    scores = jnp.einsum(
        "qhd,khd->hqk", queries, keys_all, preferred_element_type=jnp.float32
    ) * head_size ** (-0.5)
    same_image = segment_ids[:, None] == segment_ids[None, :]
    scores = jnp.where(same_image[None, :, :], scores, -1e30)
    top_score = jnp.max(scores, axis=2, keepdims=True)
    expo = jnp.exp(scores - top_score)
    attn_weights = (expo / jnp.sum(expo, axis=2, keepdims=True)).astype(jnp.bfloat16)
    context = jnp.einsum(
        "hqk,khd->qhd", attn_weights, values_all, preferred_element_type=jnp.float32
    )
    return context.reshape(row_count, model_width).astype(jnp.bfloat16)


def merge_and_place(hidden, segment_ids, owners, ln_gain, ln_bias, owner_count, capacity):
    row_count, model_width = hidden.shape
    row_mean = jnp.mean(hidden, axis=1, keepdims=True)
    centered = hidden - row_mean
    row_var = jnp.mean(centered * centered, axis=1, keepdims=True)
    normed = (centered * lax.rsqrt(row_var + 1e-06) * ln_gain[None, :] + ln_bias[None, :]).astype(
        jnp.bfloat16
    )
    merged = normed.reshape(row_count // 4, 4 * model_width)
    live_group = segment_ids.reshape(row_count // 4, 4)[:, 0] < IMGS
    group_ids = jnp.arange(row_count // 4, dtype=jnp.int32)
    earlier = (
        (owners[None, :] == owners[:, None])
        & (group_ids[None, :] < group_ids[:, None])
        & live_group[None, :]
    )
    slot_index = jnp.sum(earlier.astype(jnp.int32), axis=1)
    target = owners * capacity + slot_index
    slot_ids = jnp.arange(owner_count * capacity, dtype=jnp.int32)
    onehot_map = ((slot_ids[:, None] == target[None, :]) & live_group[None, :]).astype(jnp.bfloat16)
    return jnp.dot(onehot_map, merged, preferred_element_type=jnp.float32).astype(jnp.bfloat16)


def body(patches, query_key_value, counts, owner_index, out_weight, ln_gain, ln_bias):
    row_count, model_width = patches.shape
    owner_count = lax.axis_size("seq")
    group_count = row_count // 4
    capacity = max(2, (group_count + owner_count - 1) // owner_count)
    segment_ids = segment_rows(counts[0], row_count)
    context = attend(query_key_value, segment_ids, model_width)
    slice_rows = model_width // owner_count
    own_slice = lax.dynamic_slice_in_dim(
        out_weight, lax.axis_index("seq") * slice_rows, slice_rows, 0
    )
    weight_slab = lax.all_gather(own_slice, "dp", axis=1, tiled=True)
    projected = jnp.dot(
        context,
        lax.all_gather(weight_slab, "seq", axis=0, tiled=True),
        preferred_element_type=jnp.float32,
    )
    hidden = patches.astype(jnp.float32) + projected
    outgoing = merge_and_place(
        hidden, segment_ids, owner_index[:, 0], ln_gain, ln_bias, owner_count, capacity
    )
    outgoing = outgoing.reshape(owner_count, capacity, 4 * model_width)
    received = lax.all_to_all(outgoing, "seq", split_axis=0, concat_axis=0, tiled=True)
    return received.reshape(owner_count * capacity, 4 * model_width)


def solution(mesh):
    placed = (
        P(("dp", "seq"), None),
        P(("dp", "seq"), None),
        P(("dp", "seq"), None),
        P(("dp", "seq"), None),
        P(None, "dp"),
        P(),
        P(),
    )
    return jax.shard_map(
        body, mesh=mesh, in_specs=placed, out_specs=P(("dp", "seq"), None), check_vma=False
    )
```

profile of v0, /device:TPU:0, one launch (start us, length us, event | category | flops | bytes accessed | tf_op | source)
XLA Modules:
  0.0 86.8 jit_solution(10084298187133097372)
XLA Ops:
  6.5 1.1 %copy-done = bf16[1280,320]{0,1:T(8,128)(2,1)S(1)} copy-done((bf16[1280,320]{0,1:T(8,128)(2,1)S(1)}, bf16[1280,320]{0,1:T(8,128)(2,1)}, u32[]{:S(2)}) %copy-start) | copy-done | bytes 819224
  7.7 0.1 constant_dynamic-slice_fusion
  7.8 0.1 copy.38
  7.9 17.1 %all-gather = bf16[4,320,160]{1,2,0:T(8,128)(2,1)S(1)} all-gather(bf16[1,320,160]{1,2,0:T(8,128)(2,1)S(1)} %bitcast.29), channel_id=1, replica_groups=mesh['dp'=4,'seq'=8] {'dp'}, dimensions={0}, use_global_device_ids=true | all-gather | bytes 512000 | tf_op jit(solution)/shard_map/all_gather | solution.py:70
  25.0 0.3 copy.36
  25.3 1.1 %reshape.116 = bf16[1280,160]{0,1:T(8,128)(2,1)} reshape(bf16[4,320,160]{1,0,2:T(4,128)(2,1)S(1)} %copy.36) | data formatting | bytes 819200
  26.5 1.4 %fusion.18 = (bf16[192,1280]{1,0:T(8,128)(2,1)S(1)}, bf16[192,1280]{1,0:T(8,128)(2,1)S(1)}, bf16[192,1280]{1,0:T(8,128)(2,1)S(1)}) fusion(bf16[192,3840]{1,0:T(8,128)(2,1)} %param.8), kind=kLoop, calls=%fused_computation.34 | loop fusion | bytes 2949120 | tf_op jit(solution)/shard_map/slice | solution.py:20
  27.9 0.2 copy.31
  28.2 0.2 copy.32
  28.4 0.2 reduce-window.8
  28.6 1.1 %copy.33 = bf16[192,1280]{0,1:T(8,128)(2,1)} copy(bf16[192,1280]{1,0:T(8,128)(2,1)S(1)} %get-tuple-element.7) | data formatting | bytes 983040 | tf_op jit(solution)/shard_map/slice | solution.py:21
  29.9 0.1 fusion.13
  30.0 0.2 convert_reduce_fusion
  30.3 3.0 %fusion.19 = (f32[16,192]{1,0:T(8,128)S(1)}, f32[16,192,192]{1,2,0:T(8,128)}) fusion(pred[192,192]{0,1:T(8,128)(4,1)S(1)} %broadcast_compare_fusion, bf16[192,16,80]{0,2,1:T(8,128)(2,1)S(1)} %bitcast.26, bf16[192,16,80]{0,2,1:T(8,128)(2,1)S(1)} %bitcast.27), kind=kOutput, calls=%fused_computation.35 | convolution fusion | flops 96731328 | bytes 3391488 | tf_op jit(solution)/shard_map/sub | solution.py:28
  33.3 2.4 %fusion.6 = bf16[16,192,80]{1,2,0:T(8,128)(2,1)S(1)} fusion(bf16[192,16,80]{0,2,1:T(8,128)(2,1)S(1)} %bitcast.28, f32[16,192,192]{1,2,0:T(8,128)} %get-tuple-element.9, f32[16,192]{1,0:T(8,128)S(1)} %get-tuple-element.8), kind=kOutput, calls=%fused_computation.11 | convolution fusion | flops 95797248 | bytes 3354624 | tf_op jit(solution)/shard_map/hqk,khd->qhd/dot_general | solution.py:30
  35.7 25.4 %all-gather.3.cloned.1.call-done = bf16[1280,1280]{1,0:T(8,128)(2,1)} async-done(((bf16[160,1280]{1,0:T(8,128)(2,1)}), bf16[1280,1280]{1,0:T(8,128)(2,1)}) %all-gather.3.cloned.1.call-update) | async-done | bytes 3276816 | tf_op jit(solution)/shard_map/all_gather | solution.py:73
  61.1 2.9 %fusion.20 = (f32[192]{0:T(256)S(1)}, f32[192,1280]{1,0:T(8,128)S(1)}) fusion(bf16[192,1280]{0,1:T(8,128)(2,1)S(1)} %bitcast.25, bf16[1280,1280]{1,0:T(8,128)(2,1)} %all-gather.3.cloned.1.call-done, bf16[192,1280]{1,0:T(8,128)(2,1)S(1)} %copy-done.2), kind=kOutput, calls=%fused_computation.36 | convolution fusion | flops 629882688 | bytes 5243648 | tf_op jit(solution)/shard_map/dot_general | solution.py:71
  64.0 0.2 multiply_reduce_fusion
  64.3 0.2 add_convert_fusion
  64.6 0.3 reshape.112
  64.9 0.3 convolution_convert_fusion
  65.2 0.2 reshape.113
  65.3 13.7 %all_to_all.5 = bf16[8,6,5120]{2,1,0:T(8,128)(2,1)S(1)} all-to-all(bf16[8,6,5120]{2,1,0:T(8,128)(2,1)S(1)} %reshape.113), channel_id=1, replica_groups=mesh['dp'=4,'seq'=8] {'seq'}, dimensions={0} | all-to-all | bytes 983040 | tf_op jit(solution)/shard_map/all_to_all | solution.py:81
  79.0 1.0 %reshape.114 = bf16[48,5120]{1,0:T(8,128)(2,1)} reshape(bf16[8,6,5120]{2,1,0:T(8,128)(2,1)S(1)} %all_to_all.5) | data formatting | bytes 983040 | tf_op jit(solution)/shard_map/reshape | solution.py:82
  (21 shorter events, 0.4 us)
Async XLA Ops:
  6.5 1.1 %copy-start = (bf16[1280,320]{0,1:T(8,128)(2,1)S(1)}, bf16[1280,320]{0,1:T(8,128)(2,1)}, u32[]{:S(2)}) copy-start(bf16[1280,320]{0,1:T(8,128)(2,1)} %param.11) | copy-start | bytes 2457604
  6.5 54.6 %all-gather.3.cloned.1.call-start = ((), (), s32[]{:S(2)}) async-start(), calls=%async_computation.1 | async-start | bytes 3686400 | tf_op jit(solution)/shard_map/all_gather | solution.py:73
  25.3 3.1 %copy-start.6 = (s32[1,4]{1,0:T(1,128)S(1)}, s32[1,4]{1,0:T(1,128)}, u32[]{:S(2)}) copy-start(s32[1,4]{1,0:T(1,128)} %param.9) | copy-start | bytes 52
  26.5 3.5 %copy-start.5 = (s32[48,1]{0,1:T(1,128)S(1)}, s32[48,1]{0,1:T(1,128)}, u32[]{:S(2)}) copy-start(s32[48,1]{0,1:T(1,128)} %param.10) | copy-start | bytes 580
  30.3 3.0 %copy-start.1 = (bf16[192,1280]{0,1:T(8,128)(2,1)S(1)}, bf16[192,1280]{0,1:T(8,128)(2,1)}, u32[]{:S(2)}) copy-start(bf16[192,1280]{0,1:T(8,128)(2,1)} %copy.33) | copy-start | bytes 1474564
  33.3 27.8 %copy-start.2 = (bf16[192,1280]{1,0:T(8,128)(2,1)S(1)}, bf16[192,1280]{1,0:T(8,128)(2,1)}, u32[]{:S(2)}) copy-start(bf16[192,1280]{1,0:T(8,128)(2,1)} %param.7) | copy-start | bytes 1474564
  61.1 3.2 %copy-start.3 = (f32[1280]{0:T(1024)S(1)}, f32[1280]{0:T(1024)}, u32[]{:S(2)}) copy-start(f32[1280]{0:T(1024)} %param.13) | copy-start | bytes 15364
  61.1 3.2 %copy-start.4 = (f32[1280]{0:T(1024)S(1)}, f32[1280]{0:T(1024)}, u32[]{:S(2)}) copy-start(f32[1280]{0:T(1024)} %param.12) | copy-start | bytes 15364
Sparse Core Ops, SparseCore 0:
  26.6 34.4 all-gather.2
where the time goes:
time: 87 us; the launch traced here: 86.8 us
  blocking collectives  30.8 us (35%)
  waiting for transfers between devices  25.4 us (29%)
  between operations  13.5 us (16%)
  matrix products  8.57 us (10%)
  local copies, waits for them, and re-layouts  7.35 us (8%)
  other arithmetic  1.17 us (1%)
    all_gather x1, waiting for transfers between devices, body(): lax.all_gather(weight_slab, 'seq', axis=0, tiled=True)  25.4 us
    all_gather x1, blocking collectives, body(): weight_slab = lax.all_gather(own_slice, 'dp', axis=1, tiled=True)  17.1 us
    all_to_all x1, blocking collectives, body(): lax.all_to_all(outgoing, 'seq', split_axis=0, concat_axis=0, tiled=True)  13.7 us
    sub x1, matrix products, attend(): expo = jnp.exp(scores - top_score)  2.97 us
    dot_general x1, matrix products, body(): jnp.dot(context, lax.all_gather(weight_slab, 'seq', axis=0, tiled=True),...  2.89 us
    unnamed x16, local copies, waits for them, and re-layouts  2.45 us
    dot_general x1, matrix products, attend(): jnp.einsum('hqk,khd->qhd', attn_weights, values_all, preferred_element_ty...  2.44 us
  transfers between devices with their start and end apart: 1, of which 1 were waited for; matrix products, arithmetic and copies ran while one was open for 11% of the time, Pallas kernels for 0%

commit v1 on v0

--- a/solution.py
+++ b/solution.py
@@ -1,10 +1,15 @@
+import functools
+
 import jax
 import jax.numpy as jnp
 from jax import lax
+from jax.experimental import pallas as pl
+from jax.experimental.pallas import tpu as pltpu
 from jax.sharding import PartitionSpec as P
 
 HEADS = 16
 IMGS = 4
+MESH = pl.DeviceIdType.MESH
 
 
 def segment_rows(count_row, row_count):
@@ -56,7 +61,7 @@
     return jnp.dot(onehot_map, merged, preferred_element_type=jnp.float32).astype(jnp.bfloat16)
 
 
-def body(patches, query_key_value, counts, owner_index, out_weight, ln_gain, ln_bias):
+def plain_body(patches, query_key_value, counts, owner_index, out_weight, ln_gain, ln_bias):
     row_count, model_width = patches.shape
     owner_count = lax.axis_size("seq")
     group_count = row_count // 4
@@ -82,6 +87,331 @@
     return received.reshape(owner_count * capacity, 4 * model_width)
 
 
+def flip(index, mask):
+    bit = 1
+    while bit <= mask:
+        if mask & bit:
+            index = index + bit - 2 * bit * ((index // bit) % 2)
+        bit *= 2
+    return index
+
+
+def iota(shape, dim):
+    return lax.broadcasted_iota(jnp.int32, shape, dim)
+
+
+def fused_kernel(
+    n_dp, n_seq, capacity,
+    patches_ref, packed_ref, counts_ref, owners_ref, weight_ref, gain_ref, bias_ref,
+    landed_ref,
+    patches_v, packed_v, weight_v, context_v, outgoing_v,
+    local_sem, z_send, z_recv, p_send, p_recv, f_send, f_recv, a_send, a_recv,
+):
+    row_count, model_width = patches_ref.shape
+    head_size = model_width // HEADS
+    piece_rows = weight_ref.shape[0] // (n_seq // 2)
+    piece_lanes = model_width // 2
+    my_dp, my_seq = lax.axis_index("dp"), lax.axis_index("seq")
+    plane = list(range(2, n_seq, 2))
+    partner = flip(my_seq, 1)
+
+    load_packed = pltpu.make_async_copy(packed_ref, packed_v, local_sem.at[0])
+    load_patches = pltpu.make_async_copy(patches_ref, patches_v, local_sem.at[1])
+    load_weight = pltpu.make_async_copy(weight_ref, weight_v.at[my_dp], local_sem.at[2])
+    load_packed.start()
+    load_weight.start()
+    load_patches.start()
+
+    barrier = pltpu.get_barrier_semaphore()
+    for k in range(1, n_dp):
+        pl.semaphore_signal(
+            barrier, inc=1, device_id=(lax.rem(my_dp + k, n_dp), my_seq), device_id_type=MESH
+        )
+    for m in range(1, n_seq):
+        pl.semaphore_signal(barrier, inc=1, device_id=(my_dp, flip(my_seq, m)), device_id_type=MESH)
+    pl.semaphore_wait(barrier, n_dp + n_seq - 2)
+
+    def piece_of(ref, seq):
+        return ref.at[
+            pl.ds(pl.multiple_of((seq // 2) * piece_rows, piece_rows), piece_rows),
+            pl.ds(pl.multiple_of((seq % 2) * piece_lanes, piece_lanes), piece_lanes),
+        ]
+
+    z_copies = []
+    for k in range(1, n_dp):
+        copy = pltpu.make_async_remote_copy(
+            src_ref=piece_of(weight_ref, my_seq),
+            dst_ref=piece_of(weight_v.at[my_dp], my_seq),
+            send_sem=z_send.at[k - 1],
+            recv_sem=z_recv.at[k - 1],
+            device_id=(lax.rem(my_dp + k, n_dp), my_seq),
+            device_id_type=MESH,
+        )
+        copy.start()
+        z_copies.append(copy)
+
+    def piece_copy(k, seq_of_rows, target, send_sem, recv_sem):
+        piece = piece_of(weight_v.at[lax.rem(my_dp + n_dp - k, n_dp)], seq_of_rows)
+        return pltpu.make_async_remote_copy(
+            src_ref=piece, dst_ref=piece, send_sem=send_sem, recv_sem=recv_sem,
+            device_id=(my_dp, target), device_id_type=MESH,
+        )
+
+    p_copies, f_copies = {}, {}
+
+    def spread(k):
+        z_copies[k - 1].wait_recv()
+        for i, m in enumerate(plane + [1]):
+            copy = piece_copy(
+                k, my_seq, flip(my_seq, m), p_send.at[k - 1, i], p_recv.at[k - 1, i]
+            )
+            copy.start()
+            p_copies[k, i] = copy
+
+    def forward(k, i):
+        p_copies[k, i].wait_recv()
+        copy = piece_copy(
+            k, flip(my_seq, plane[i]), partner, f_send.at[k - 1, i], f_recv.at[k - 1, i]
+        )
+        copy.start()
+        f_copies[k, i] = copy
+
+    hooks = [functools.partial(spread, k) for k in range(1, n_dp)]
+
+    load_packed.wait()
+    ends, total = [], 0
+    for i in range(IMGS):
+        total = total + counts_ref[0, i]
+        ends.append(total)
+
+    def segments(shape, dim):
+        ids = iota(shape, dim)
+        found = jnp.zeros(shape, jnp.int32)
+        for end in ends:
+            found = found + (ids >= end).astype(jnp.int32)
+        return found
+
+    same = segments((row_count, row_count), 0) == segments((row_count, row_count), 1)
+    scale = head_size ** (-0.5)
+    pending = None
+    pending_at = 0
+    for head in range(HEADS):
+        first, last = head * head_size, (head + 1) * head_size
+        low, high = first // 128 * 128, -(-last // 128) * 128
+        lanes = iota((row_count, high - low), 1)
+        mine = (lanes >= first - low) & (lanes < last - low)
+        queries = packed_v[:, low:high]
+        queries = jnp.where(mine, queries, jnp.zeros_like(queries))
+        scores = lax.dot_general(
+            queries, packed_v[:, model_width + low : model_width + high],
+            (((1,), (1,)), ((), ())), preferred_element_type=jnp.float32,
+        )
+        scores = jnp.where(same, scores, -1e30)
+        top_score = jnp.max(scores, axis=1, keepdims=True)
+        expo = jnp.exp((scores - top_score) * scale)
+        weights = (expo * (1.0 / jnp.sum(expo, axis=1, keepdims=True))).astype(jnp.bfloat16)
+        found = jnp.dot(
+            weights, packed_v[:, 2 * model_width + low : 2 * model_width + high],
+            preferred_element_type=jnp.float32,
+        )
+        found = jnp.where(mine, found, 0.0)
+        if pending is not None and pending_at > low:
+            shared = pending_at - low
+            if shared > 0:
+                head_part = pending + found[:, :shared]
+                found = (
+                    jnp.concatenate([head_part, found[:, shared:]], axis=1)
+                    if shared < high - low else head_part
+                )
+        done = last // 128 * 128
+        if done > low:
+            context_v[:, low:done] = found[:, : done - low].astype(jnp.bfloat16)
+        if done < high:
+            pending, pending_at = found[:, done - low :], high
+        else:
+            pending = None
+        if hooks and head % 3 == 2:
+            hooks.pop(0)()
+    while hooks:
+        hooks.pop(0)()
+    for k in range(1, n_dp):
+        for i in range(len(plane)):
+            forward(k, i)
+
+    load_weight.wait()
+    load_patches.wait()
+    for k in range(1, n_dp):
+        p_copies[k, len(plane)].wait_recv()
+        for i in range(len(plane)):
+            f_copies[k, i].wait_recv()
+    context = context_v[...]
+    hidden = patches_v[...].astype(jnp.float32) + jnp.concatenate(
+        [
+            lax.dot_general(
+                context, weight_v[d], (((1,), (1,)), ((), ())),
+                preferred_element_type=jnp.float32,
+            )
+            for d in range(n_dp)
+        ],
+        axis=1,
+    )
+    row_mean = jnp.mean(hidden, axis=1, keepdims=True)
+    centered = hidden - row_mean
+    row_var = jnp.mean(centered * centered, axis=1, keepdims=True)
+    normed = (
+        centered * lax.rsqrt(row_var + 1e-06) * gain_ref[...].reshape(1, model_width)
+        + bias_ref[...].reshape(1, model_width)
+    ).astype(jnp.bfloat16)
+
+    group_count = row_count // 4
+    diagonal = iota((group_count, group_count), 0) == iota((group_count, group_count), 1)
+    owners = jnp.sum(jnp.where(diagonal, owners_ref[...], 0), axis=1, keepdims=True)
+    groups = iota((group_count, row_count), 0)
+    group_of_row = iota((group_count, row_count), 1) >> 2
+    owner_of_row = jnp.sum(jnp.where(groups == group_of_row, owners, 0), axis=0, keepdims=True)
+    earlier = (owners == owner_of_row) & (groups < group_of_row) & (groups * 4 < total)
+    slot_of_row = jnp.sum(earlier.astype(jnp.int32), axis=0, keepdims=True)
+    block_rows = 4 * capacity
+    row_ids = iota((1, row_count), 1)
+    place = owner_of_row * block_rows + slot_of_row * 4 + (row_ids & 3)
+    place = jnp.where((row_ids >> 2) * 4 < total, place, -1)
+    tall = n_seq * 16
+    lines = iota((tall, row_count), 0)
+    half = model_width // 2
+    for f in range(block_rows // 16):
+        chosen = ((lines >> 4) * block_rows + 16 * f + (lines & 15) == place).astype(jnp.bfloat16)
+        placed = jnp.dot(chosen, normed, preferred_element_type=jnp.float32).astype(jnp.bfloat16)
+        outgoing_v[:, :, f * model_width : (f + 1) * model_width] = placed.reshape(
+            n_seq, 16, model_width
+        )
+    if block_rows % 16:
+        f = block_rows // 16
+        chosen = ((lines >> 4) * block_rows + 16 * f + (lines & 7) == place).astype(jnp.bfloat16)
+        placed = jnp.dot(chosen, normed, preferred_element_type=jnp.float32)
+        upper = (iota((tall, half), 0) & 15) < 8
+        placed = jnp.where(upper, placed[:, :half], placed[:, half:]).astype(jnp.bfloat16)
+        outgoing_v[:, :, f * model_width :] = placed.reshape(n_seq, 16, half)
+
+    a_copies = []
+    for m in plane[::-1] + [0] + [m + 1 for m in plane[::-1]] + [1]:
+        target = flip(my_seq, m)
+        if m == 0:
+            continue
+        copy = pltpu.make_async_remote_copy(
+            src_ref=outgoing_v.at[target],
+            dst_ref=landed_ref.at[my_seq],
+            send_sem=a_send.at[m - 1],
+            recv_sem=a_recv.at[m - 1],
+            device_id=(my_dp, target),
+            device_id_type=MESH,
+        )
+        copy.start()
+        a_copies.append(copy)
+    keep = pltpu.make_async_copy(outgoing_v.at[my_seq], landed_ref.at[my_seq], local_sem.at[3])
+    keep.start()
+    for copy in z_copies + list(p_copies.values()) + list(f_copies.values()):
+        copy.wait_send()
+    keep.wait()
+    for copy in a_copies:
+        copy.wait()
+
+
+def layout_kernel(capacity, landed_ref, out_ref):
+    n_seq, _, lanes = landed_ref.shape
+    model_width = out_ref.shape[1] // 4
+    half = model_width // 2
+    block_rows = 4 * capacity
+    out_rows = n_seq * capacity
+    landed = landed_ref[...].reshape(n_seq * 16, lanes)
+    rows = iota((out_rows, n_seq * 16), 0)
+    lines = iota((out_rows, n_seq * 16), 1)
+    full = block_rows // 16
+
+    def pick(first, line, j, keep):
+        spot = first + line
+        return (
+            (rows == (lines >> 4) * capacity + (spot >> 2)) & ((spot & 3) == j) & keep
+        ).astype(jnp.bfloat16)
+
+    always = lines >= 0
+    for j in range(4):
+        left = jnp.zeros((out_rows, half), jnp.float32)
+        right = jnp.zeros((out_rows, half), jnp.float32)
+        for f in range(full):
+            part = jnp.dot(
+                pick(16 * f, lines & 15, j, always),
+                landed[:, f * model_width : (f + 1) * model_width],
+                preferred_element_type=jnp.float32,
+            )
+            left, right = left + part[:, :half], right + part[:, half:]
+        if block_rows % 16:
+            tail = landed[:, full * model_width :]
+            left = left + jnp.dot(
+                pick(16 * full, lines & 7, j, (lines & 15) < 8), tail,
+                preferred_element_type=jnp.float32,
+            )
+            right = right + jnp.dot(
+                pick(16 * full, lines & 7, j, (lines & 15) >= 8), tail,
+                preferred_element_type=jnp.float32,
+            )
+        out_ref[:, j * model_width : j * model_width + half] = left.astype(jnp.bfloat16)
+        out_ref[:, j * model_width + half : (j + 1) * model_width] = right.astype(jnp.bfloat16)
+
+
+def fused_body(patches, query_key_value, counts, owner_index, out_weight, ln_gain, ln_bias):
+    row_count, model_width = patches.shape
+    n_dp, n_seq = lax.axis_size("dp"), lax.axis_size("seq")
+    capacity = max(2, (row_count // 4 + n_seq - 1) // n_seq)
+    planes = n_seq // 2 - 1
+    block_lanes = model_width * 4 * capacity // 16
+    any_spec = pl.BlockSpec(memory_space=pl.ANY)
+    vmem_spec = pl.BlockSpec(memory_space=pltpu.VMEM)
+    dma = pltpu.SemaphoreType.DMA
+    landed = pl.pallas_call(
+        functools.partial(fused_kernel, n_dp, n_seq, capacity),
+        out_shape=jax.ShapeDtypeStruct((n_seq, 16, block_lanes), jnp.bfloat16),
+        in_specs=[
+            any_spec, any_spec, pl.BlockSpec(memory_space=pltpu.SMEM), vmem_spec, any_spec,
+            vmem_spec, vmem_spec,
+        ],
+        out_specs=vmem_spec,
+        scratch_shapes=[
+            pltpu.VMEM(patches.shape, jnp.bfloat16),
+            pltpu.VMEM(query_key_value.shape, jnp.bfloat16),
+            pltpu.VMEM((n_dp,) + out_weight.shape[::-1], jnp.bfloat16),
+            pltpu.VMEM(patches.shape, jnp.bfloat16),
+            pltpu.VMEM((n_seq, 16, block_lanes), jnp.bfloat16),
+            dma((4,)),
+            dma((n_dp - 1,)), dma((n_dp - 1,)),
+            dma((n_dp - 1, planes + 1)), dma((n_dp - 1, planes + 1)),
+            dma((n_dp - 1, planes)), dma((n_dp - 1, planes)),
+            dma((n_seq - 1,)), dma((n_seq - 1,)),
+        ],
+        compiler_params=pltpu.CompilerParams(
+            collective_id=0, has_side_effects=True
+        ),
+        name="fused",
+    )(
+        patches, query_key_value, counts, owner_index.T, out_weight.T,
+        ln_gain, ln_bias,
+    )
+    return pl.pallas_call(
+        functools.partial(layout_kernel, capacity),
+        out_shape=jax.ShapeDtypeStruct((n_seq * capacity, 4 * model_width), jnp.bfloat16),
+        in_specs=[vmem_spec],
+        out_specs=vmem_spec,
+        compiler_params=pltpu.CompilerParams(vmem_limit_bytes=16 * 1024 * 1024),
+        name="layout",
+    )(landed)
+
+
+def body(patches, query_key_value, counts, owner_index, out_weight, ln_gain, ln_bias):
+    n_seq = lax.axis_size("seq")
+    whole_tiles = out_weight.shape[1] % (8 * n_seq) == 0 and n_seq & (n_seq - 1) == 0
+    run = fused_body if whole_tiles else plain_body
+    return run(patches, query_key_value, counts, owner_index, out_weight, ln_gain, ln_bias)
+
+
 def solution(mesh):
     placed = (
         P(("dp", "seq"), None),

time: 87 us -> 40.5 us (0.47)
  Pallas kernels: 0 us -> 39.3 us
  blocking collectives: 30.8 us -> 0 us
  waiting for transfers between devices: 25.4 us -> 0 us
  between operations: 13.5 us -> 0.02 us
  matrix products: 8.57 us -> 0 us
  local copies, waits for them, and re-layouts: 7.35 us -> 1.02 us
  other arithmetic: 1.17 us -> 0 us
    pallas_call x0 -> x2, Pallas kernels: none -> 39.3 us  [the longest x1 38 us: fused_body(): pl.pallas_call(functools.partial(fused_kernel, n_dp, n_seq, capacity), ou...]
    all_gather x1 -> x0, waiting for transfers between devices: 25.4 us -> none  [body(): lax.all_gather(weight_slab, 'seq', axis=0, tiled=True)]
    all_gather x1 -> x0, blocking collectives: 17.1 us -> none  [body(): weight_slab = lax.all_gather(own_slice, 'dp', axis=1, tiled=True)]
    all_to_all x1 -> x0, blocking collectives: 13.7 us -> none  [body(): lax.all_to_all(outgoing, 'seq', split_axis=0, concat_axis=0, tiled=True)]
    dot_general x3 -> x0, matrix products: 5.6 us -> none  [the longest x1 2.89 us: body(): jnp.dot(context, lax.all_gather(weight_slab, 'seq', axis=0, tiled=True),...]
    slice x4 -> x0, local copies, waits for them, and re-layouts: 3 us -> none  [the longest x2 1.67 us: attend(): packed[:, model_width:2 * model_width].reshape(row_count, HEADS, head_size)]
    sub x1 -> x0, matrix products: 2.97 us -> none  [attend(): expo = jnp.exp(scores - top_score)]
    reshape x4 -> x0, local copies, waits for them, and re-layouts: 1.53 us -> none  [the longest x1 0.95 us: body(): return received.reshape(owner_count * capacity, 4 * model_width)]
  transfers between devices with their start and end apart: 1 -> 0, of which waited for: 1 -> 0; matrix products, arithmetic and copies ran while one was open for 11% -> 0% of each run, Pallas kernels for 0% -> 0%
where the time goes in v1:
time: 40.5 us; the launch traced here: 40.3 us
  Pallas kernels  39.3 us (97%)
  local copies, waits for them, and re-layouts  1.02 us (3%)
    pallas_call x1, Pallas kernels, fused_body(): pl.pallas_call(functools.partial(fused_kernel, n_dp, n_seq, capacity), ou...  38 us
    pallas_call x1, Pallas kernels, fused_body(): pl.pallas_call(functools.partial(layout_kernel, capacity), out_shape=jax....  1.3 us
    unnamed x2, local copies, waits for them, and re-layouts  1.02 us

profile of v1, /device:TPU:0, one launch (start us, length us, event | category | flops | bytes accessed | tf_op | source)
XLA Modules:
  0.0 40.3 jit_solution(15634117927984212043)
XLA Ops:
  0.0 38.0 %fused.1.landed_ref = bf16[8,16,1920]{2,1,0:T(8,128)(2,1)} custom-call(bf16[192,1280]{1,0:T(8,128)(2,1)} %patches_ref.1, bf16[192,3840]{1,0:T(8,128)(2,1)} %packed_ref.1, s32[1,4]{1,0:T(1,128)} %counts_ref.1, s32[1,48]{1,0:T(1,128)} %bitcast.3, bf16[320,1280]{1,0:T(8,128)(2,1)} %bitcast.2, f32[1280]{0:T(1024)} %gain_ref.1, f32[1280]{0:T(1024)} %bias_ref.1), custom_call_target="tpu_custom_call" | custom-call | tf_op jit(solution)/shard_map/fused/pallas_call | solution.py:370
  38.0 0.0 copy-start
  38.0 1.0 %copy-done = bf16[8,16,1920]{2,1,0:T(8,128)(2,1)S(1)} copy-done((bf16[8,16,1920]{2,1,0:T(8,128)(2,1)S(1)}, bf16[8,16,1920]{2,1,0:T(8,128)(2,1)}, u32[]{:S(2)}) %copy-start) | copy-done | bytes 491544
  39.0 1.3 %layout.1 = bf16[48,5120]{1,0:T(8,128)(2,1)} custom-call(bf16[8,16,1920]{2,1,0:T(8,128)(2,1)S(1)} %copy-done), custom_call_target="tpu_custom_call" | custom-call | tf_op jit(solution)/shard_map/layout/pallas_call | solution.py:398
Async XLA Ops:
  38.0 1.0 %copy-start = (bf16[8,16,1920]{2,1,0:T(8,128)(2,1)S(1)}, bf16[8,16,1920]{2,1,0:T(8,128)(2,1)}, u32[]{:S(2)}) copy-start(bf16[8,16,1920]{2,1,0:T(8,128)(2,1)} %fused.1.landed_ref) | copy-start | bytes 1474564

commit v2 on v1

--- a/solution.py
+++ b/solution.py
@@ -104,8 +104,8 @@
     n_dp, n_seq, capacity,
     patches_ref, packed_ref, counts_ref, owners_ref, weight_ref, gain_ref, bias_ref,
     landed_ref,
-    patches_v, packed_v, weight_v, context_v, outgoing_v,
-    local_sem, z_send, z_recv, p_send, p_recv, f_send, f_recv, a_send, a_recv,
+    patches_v, packed_v, weight_v, context_v, projected_v, outgoing_v,
+    local_sem, z_send, z_recv, p_send, p_recv, a_send, a_recv,
 ):
     row_count, model_width = patches_ref.shape
     head_size = model_width // HEADS
@@ -137,46 +137,76 @@
             pl.ds(pl.multiple_of((seq % 2) * piece_lanes, piece_lanes), piece_lanes),
         ]
 
-    z_copies = []
-    for k in range(1, n_dp):
+    def at_dp(table):
+        return sum(
+            entry * (1 - ((my_dp - i + n_dp) % n_dp + n_dp - 1) // n_dp)
+            for i, entry in enumerate(table)
+        )
+
+    orders = [
+        sorted((e for e in range(n_dp) if e != d), key=lambda e: (abs(e - d), e))
+        for d in range(n_dp)
+    ]
+    rounds = range(n_dp - 1)
+    sources = [at_dp([order[r] for order in orders]) for r in rounds]
+    core = my_seq % 2
+    x_side, y_side = flip(my_seq, 2), flip(my_seq, 4)
+    side_a = (1 - core) * x_side + core * y_side
+    side_b = core * x_side + (1 - core) * y_side
+    far_side = flip(my_seq, 6)
+
+    def z_copy(r, owner_dp):
+        return pltpu.make_async_remote_copy(
+            src_ref=piece_of(weight_ref, my_seq),
+            dst_ref=piece_of(weight_v.at[owner_dp], my_seq),
+            send_sem=z_send.at[r],
+            recv_sem=z_recv.at[owner_dp],
+            device_id=(sources[r], my_seq),
+            device_id_type=MESH,
+        )
+
+    z_copies = [z_copy(r, my_dp) for r in rounds]
+    for copy in z_copies:
+        copy.start()
+
+    sent = {}
+
+    def send_piece(r, kind, seq_of_rows, target):
+        piece = piece_of(weight_v.at[sources[r]], seq_of_rows)
         copy = pltpu.make_async_remote_copy(
-            src_ref=piece_of(weight_ref, my_seq),
-            dst_ref=piece_of(weight_v.at[my_dp], my_seq),
-            send_sem=z_send.at[k - 1],
-            recv_sem=z_recv.at[k - 1],
-            device_id=(lax.rem(my_dp + k, n_dp), my_seq),
-            device_id_type=MESH,
+            src_ref=piece, dst_ref=piece, send_sem=p_send.at[r, kind], recv_sem=p_recv.at[r, kind],
+            device_id=(my_dp, target), device_id_type=MESH,
         )
         copy.start()
-        z_copies.append(copy)
-
-    def piece_copy(k, seq_of_rows, target, send_sem, recv_sem):
-        piece = piece_of(weight_v.at[lax.rem(my_dp + n_dp - k, n_dp)], seq_of_rows)
-        return pltpu.make_async_remote_copy(
-            src_ref=piece, dst_ref=piece, send_sem=send_sem, recv_sem=recv_sem,
-            device_id=(my_dp, target), device_id_type=MESH,
-        )
-
-    p_copies, f_copies = {}, {}
-
-    def spread(k):
-        z_copies[k - 1].wait_recv()
-        for i, m in enumerate(plane + [1]):
-            copy = piece_copy(
-                k, my_seq, flip(my_seq, m), p_send.at[k - 1, i], p_recv.at[k - 1, i]
-            )
-            copy.start()
-            p_copies[k, i] = copy
-
-    def forward(k, i):
-        p_copies[k, i].wait_recv()
-        copy = piece_copy(
-            k, flip(my_seq, plane[i]), partner, f_send.at[k - 1, i], f_recv.at[k - 1, i]
-        )
-        copy.start()
-        f_copies[k, i] = copy
-
-    hooks = [functools.partial(spread, k) for k in range(1, n_dp)]
+        sent[r, kind] = copy
+
+    def from_z(r):
+        z_copy(r, sources[r]).wait_recv()
+        send_piece(r, 0, my_seq, side_a)
+        send_piece(r, 1, my_seq, side_b)
+        send_piece(r, 3, my_seq, partner)
+
+    def from_sides(r):
+        sent[r, 0].wait_recv()
+        send_piece(r, 2, side_a, side_b)
+        send_piece(r, 4, side_a, partner)
+        sent[r, 1].wait_recv()
+        send_piece(r, 5, side_b, partner)
+
+    def from_far(r):
+        sent[r, 2].wait_recv()
+        send_piece(r, 6, far_side, partner)
+
+    def project(dp):
+        projected_v[dp] = lax.dot_general(
+            context_v[...], weight_v[dp], (((1,), (1,)), ((), ())),
+            preferred_element_type=jnp.float32,
+        )
+
+    def finish(r):
+        for kind in range(3, 7):
+            sent[r, kind].wait_recv()
+        project(sources[r])
 
     load_packed.wait()
     ends, total = [], 0
@@ -230,30 +260,21 @@
             pending, pending_at = found[:, done - low :], high
         else:
             pending = None
-        if hooks and head % 3 == 2:
-            hooks.pop(0)()
-    while hooks:
-        hooks.pop(0)()
-    for k in range(1, n_dp):
-        for i in range(len(plane)):
-            forward(k, i)
 
     load_weight.wait()
+    project(my_dp)
     load_patches.wait()
-    for k in range(1, n_dp):
-        p_copies[k, len(plane)].wait_recv()
-        for i in range(len(plane)):
-            f_copies[k, i].wait_recv()
-    context = context_v[...]
+    for step in range(n_dp + 2):
+        if step < n_dp - 1:
+            from_z(step)
+        if 1 <= step < n_dp:
+            from_sides(step - 1)
+        if 2 <= step < n_dp + 1:
+            from_far(step - 2)
+        if 3 <= step:
+            finish(step - 3)
     hidden = patches_v[...].astype(jnp.float32) + jnp.concatenate(
-        [
-            lax.dot_general(
-                context, weight_v[d], (((1,), (1,)), ((), ())),
-                preferred_element_type=jnp.float32,
-            )
-            for d in range(n_dp)
-        ],
-        axis=1,
+        [projected_v[d] for d in range(n_dp)], axis=1
     )
     row_mean = jnp.mean(hidden, axis=1, keepdims=True)
     centered = hidden - row_mean
@@ -309,7 +330,7 @@
         a_copies.append(copy)
     keep = pltpu.make_async_copy(outgoing_v.at[my_seq], landed_ref.at[my_seq], local_sem.at[3])
     keep.start()
-    for copy in z_copies + list(p_copies.values()) + list(f_copies.values()):
+    for copy in z_copies + list(sent.values()):
         copy.wait_send()
     keep.wait()
     for copy in a_copies:
@@ -362,7 +383,6 @@
     row_count, model_width = patches.shape
     n_dp, n_seq = lax.axis_size("dp"), lax.axis_size("seq")
     capacity = max(2, (row_count // 4 + n_seq - 1) // n_seq)
-    planes = n_seq // 2 - 1
     block_lanes = model_width * 4 * capacity // 16
     any_spec = pl.BlockSpec(memory_space=pl.ANY)
     vmem_spec = pl.BlockSpec(memory_space=pltpu.VMEM)
@@ -380,11 +400,11 @@
             pltpu.VMEM(query_key_value.shape, jnp.bfloat16),
             pltpu.VMEM((n_dp,) + out_weight.shape[::-1], jnp.bfloat16),
             pltpu.VMEM(patches.shape, jnp.bfloat16),
+            pltpu.VMEM((n_dp, row_count, out_weight.shape[1]), jnp.float32),
             pltpu.VMEM((n_seq, 16, block_lanes), jnp.bfloat16),
             dma((4,)),
-            dma((n_dp - 1,)), dma((n_dp - 1,)),
-            dma((n_dp - 1, planes + 1)), dma((n_dp - 1, planes + 1)),
-            dma((n_dp - 1, planes)), dma((n_dp - 1, planes)),
+            dma((n_dp - 1,)), dma((n_dp,)),
+            dma((n_dp - 1, 7)), dma((n_dp - 1, 7)),
             dma((n_seq - 1,)), dma((n_seq - 1,)),
         ],
         compiler_params=pltpu.CompilerParams(
@@ -407,8 +427,8 @@
 
 def body(patches, query_key_value, counts, owner_index, out_weight, ln_gain, ln_bias):
     n_seq = lax.axis_size("seq")
-    whole_tiles = out_weight.shape[1] % (8 * n_seq) == 0 and n_seq & (n_seq - 1) == 0
-    run = fused_body if whole_tiles else plain_body
+    square = n_seq == 2 * 2 * 2 and out_weight.shape[1] % (8 * n_seq) == 0
+    run = fused_body if square else plain_body
     return run(patches, query_key_value, counts, owner_index, out_weight, ln_gain, ln_bias)
 
 

time: 40.5 us -> 41.2 us (1.017)
  Pallas kernels: 39.3 us -> 39.9 us
    pallas_call x1, Pallas kernels: 38 us -> 38.6 us  [fused_body(): pl.pallas_call(functools.partial(fused_kernel, n_dp, n_seq, capacity), ou...]
where the time goes in v2:
time: 41.2 us; the launch traced here: 41 us
  Pallas kernels  39.9 us (97%)
  local copies, waits for them, and re-layouts  1.02 us (2%)
    pallas_call x1, Pallas kernels, fused_body(): pl.pallas_call(functools.partial(fused_kernel, n_dp, n_seq, capacity), ou...  38.6 us
    pallas_call x1, Pallas kernels, fused_body(): pl.pallas_call(functools.partial(layout_kernel, capacity), out_shape=jax....  1.3 us
    unnamed x2, local copies, waits for them, and re-layouts  1.02 us

profile of v2, /device:TPU:0, one launch (start us, length us, event | category | flops | bytes accessed | tf_op | source)
XLA Modules:
  0.0 41.0 jit_solution(6530684229608634919)
XLA Ops:
  0.0 38.6 %fused.1.landed_ref = bf16[8,16,1920]{2,1,0:T(8,128)(2,1)} custom-call(bf16[192,1280]{1,0:T(8,128)(2,1)} %patches_ref.1, bf16[192,3840]{1,0:T(8,128)(2,1)} %packed_ref.1, s32[1,4]{1,0:T(1,128)} %counts_ref.1, s32[1,48]{1,0:T(1,128)} %bitcast.3, bf16[320,1280]{1,0:T(8,128)(2,1)} %bitcast.2, f32[1280]{0:T(1024)} %gain_ref.1, f32[1280]{0:T(1024)} %bias_ref.1), custom_call_target="tpu_custom_call" | custom-call | tf_op jit(solution)/shard_map/fused/pallas_call | solution.py:390
  38.6 0.0 copy-start
  38.7 1.0 %copy-done = bf16[8,16,1920]{2,1,0:T(8,128)(2,1)S(1)} copy-done((bf16[8,16,1920]{2,1,0:T(8,128)(2,1)S(1)}, bf16[8,16,1920]{2,1,0:T(8,128)(2,1)}, u32[]{:S(2)}) %copy-start) | copy-done | bytes 491544
  39.7 1.3 %layout.1 = bf16[48,5120]{1,0:T(8,128)(2,1)} custom-call(bf16[8,16,1920]{2,1,0:T(8,128)(2,1)S(1)} %copy-done), custom_call_target="tpu_custom_call" | custom-call | tf_op jit(solution)/shard_map/layout/pallas_call | solution.py:418
Async XLA Ops:
  38.6 1.0 %copy-start = (bf16[8,16,1920]{2,1,0:T(8,128)(2,1)S(1)}, bf16[8,16,1920]{2,1,0:T(8,128)(2,1)}, u32[]{:S(2)}) copy-start(bf16[8,16,1920]{2,1,0:T(8,128)(2,1)} %fused.1.landed_ref) | copy-start | bytes 1474564

commit v3 on v2

--- a/solution.py
+++ b/solution.py
@@ -131,10 +131,14 @@
         pl.semaphore_signal(barrier, inc=1, device_id=(my_dp, flip(my_seq, m)), device_id_type=MESH)
     pl.semaphore_wait(barrier, n_dp + n_seq - 2)
 
-    def piece_of(ref, seq):
+    first_lanes = piece_lanes // 256 * 128
+
+    def piece_of(ref, seq, part):
+        skip = part * first_lanes
+        width = piece_lanes - first_lanes if part else first_lanes
         return ref.at[
             pl.ds(pl.multiple_of((seq // 2) * piece_rows, piece_rows), piece_rows),
-            pl.ds(pl.multiple_of((seq % 2) * piece_lanes, piece_lanes), piece_lanes),
+            pl.ds(pl.multiple_of((seq % 2) * piece_lanes + skip, 128), width),
         ]
 
     def at_dp(table):
@@ -147,8 +151,8 @@
         sorted((e for e in range(n_dp) if e != d), key=lambda e: (abs(e - d), e))
         for d in range(n_dp)
     ]
-    rounds = range(n_dp - 1)
-    sources = [at_dp([order[r] for order in orders]) for r in rounds]
+    rounds = range(2 * (n_dp - 1))
+    sources = [at_dp([order[r // 2] for order in orders]) for r in rounds]
     core = my_seq % 2
     x_side, y_side = flip(my_seq, 2), flip(my_seq, 4)
     side_a = (1 - core) * x_side + core * y_side
@@ -157,10 +161,10 @@
 
     def z_copy(r, owner_dp):
         return pltpu.make_async_remote_copy(
-            src_ref=piece_of(weight_ref, my_seq),
-            dst_ref=piece_of(weight_v.at[owner_dp], my_seq),
+            src_ref=piece_of(weight_ref, my_seq, r % 2),
+            dst_ref=piece_of(weight_v.at[owner_dp], my_seq, r % 2),
             send_sem=z_send.at[r],
-            recv_sem=z_recv.at[owner_dp],
+            recv_sem=z_recv.at[owner_dp, r % 2],
             device_id=(sources[r], my_seq),
             device_id_type=MESH,
         )
@@ -172,7 +176,7 @@
     sent = {}
 
     def send_piece(r, kind, seq_of_rows, target):
-        piece = piece_of(weight_v.at[sources[r]], seq_of_rows)
+        piece = piece_of(weight_v.at[sources[r]], seq_of_rows, r % 2)
         copy = pltpu.make_async_remote_copy(
             src_ref=piece, dst_ref=piece, send_sem=p_send.at[r, kind], recv_sem=p_recv.at[r, kind],
             device_id=(my_dp, target), device_id_type=MESH,
@@ -206,7 +210,8 @@
     def finish(r):
         for kind in range(3, 7):
             sent[r, kind].wait_recv()
-        project(sources[r])
+        if r % 2:
+            project(sources[r])
 
     load_packed.wait()
     ends, total = [], 0
@@ -264,12 +269,12 @@
     load_weight.wait()
     project(my_dp)
     load_patches.wait()
-    for step in range(n_dp + 2):
-        if step < n_dp - 1:
+    for step in range(len(rounds) + 3):
+        if step < len(rounds):
             from_z(step)
-        if 1 <= step < n_dp:
+        if 1 <= step <= len(rounds):
             from_sides(step - 1)
-        if 2 <= step < n_dp + 1:
+        if 2 <= step <= len(rounds) + 1:
             from_far(step - 2)
         if 3 <= step:
             finish(step - 3)
@@ -403,8 +408,8 @@
             pltpu.VMEM((n_dp, row_count, out_weight.shape[1]), jnp.float32),
             pltpu.VMEM((n_seq, 16, block_lanes), jnp.bfloat16),
             dma((4,)),
-            dma((n_dp - 1,)), dma((n_dp,)),
-            dma((n_dp - 1, 7)), dma((n_dp - 1, 7)),
+            dma((2 * (n_dp - 1),)), dma((n_dp, 2)),
+            dma((2 * (n_dp - 1), 7)), dma((2 * (n_dp - 1), 7)),
             dma((n_seq - 1,)), dma((n_seq - 1,)),
         ],
         compiler_params=pltpu.CompilerParams(

time: 41.2 us -> 43.1 us (1.046)
  Pallas kernels: 39.9 us -> 41.9 us
    pallas_call x1, Pallas kernels: 38.6 us -> 40.6 us  [fused_body(): pl.pallas_call(functools.partial(fused_kernel, n_dp, n_seq, capacity), ou...]
where the time goes in v3:
time: 43.1 us; the launch traced here: 42.9 us
  Pallas kernels  41.9 us (97%)
  local copies, waits for them, and re-layouts  1.02 us (2%)
    pallas_call x1, Pallas kernels, fused_body(): pl.pallas_call(functools.partial(fused_kernel, n_dp, n_seq, capacity), ou...  40.6 us
    pallas_call x1, Pallas kernels, fused_body(): pl.pallas_call(functools.partial(layout_kernel, capacity), out_shape=jax....  1.3 us
    unnamed x2, local copies, waits for them, and re-layouts  1.02 us

profile of v3, /device:TPU:0, one launch (start us, length us, event | category | flops | bytes accessed | tf_op | source)
XLA Modules:
  0.0 42.9 jit_solution(7755101425639523472)
XLA Ops:
  0.0 40.6 %fused.1.landed_ref = bf16[8,16,1920]{2,1,0:T(8,128)(2,1)} custom-call(bf16[192,1280]{1,0:T(8,128)(2,1)} %patches_ref.1, bf16[192,3840]{1,0:T(8,128)(2,1)} %packed_ref.1, s32[1,4]{1,0:T(1,128)} %counts_ref.1, s32[1,48]{1,0:T(1,128)} %bitcast.3, bf16[320,1280]{1,0:T(8,128)(2,1)} %bitcast.2, f32[1280]{0:T(1024)} %gain_ref.1, f32[1280]{0:T(1024)} %bias_ref.1), custom_call_target="tpu_custom_call" | custom-call | tf_op jit(solution)/shard_map/fused/pallas_call | solution.py:395
  40.6 0.0 copy-start
  40.6 1.0 %copy-done = bf16[8,16,1920]{2,1,0:T(8,128)(2,1)S(1)} copy-done((bf16[8,16,1920]{2,1,0:T(8,128)(2,1)S(1)}, bf16[8,16,1920]{2,1,0:T(8,128)(2,1)}, u32[]{:S(2)}) %copy-start) | copy-done | bytes 491544
  41.6 1.3 %layout.1 = bf16[48,5120]{1,0:T(8,128)(2,1)} custom-call(bf16[8,16,1920]{2,1,0:T(8,128)(2,1)S(1)} %copy-done), custom_call_target="tpu_custom_call" | custom-call | tf_op jit(solution)/shard_map/layout/pallas_call | solution.py:423
Async XLA Ops:
  40.6 1.0 %copy-start = (bf16[8,16,1920]{2,1,0:T(8,128)(2,1)S(1)}, bf16[8,16,1920]{2,1,0:T(8,128)(2,1)}, u32[]{:S(2)}) copy-start(bf16[8,16,1920]{2,1,0:T(8,128)(2,1)} %fused.1.landed_ref) | copy-start | bytes 1474564
